TPU v7x, 32 devices: a whole 2x2x4 slice. The times are simulated.
32 devices in a mesh: row: 4 (over y, x), col: 8 (over z, core).
Axes of the slice: x: 2, y: 2, z: 4, core: 2. Of those that a mesh axis runs over, the one named last changes fastest.
Arguments:
- teacher: bfloat16 [16384, 256], replicated, may hold values from -4 to 4
- panel_ids: int32 [2048], P('col'), may hold values from 0 to 16383
- rest_ids: int32 [4, 8, 128], P('row', 'col'), may hold values from 0 to 16383
- inverse: bfloat16 [2048, 2048], replicated, may hold values from -1 to 1, as said below
Outputs:
- trailing: float32 [8, 4, 128, 4, 8, 128], P(None, 'row', None, None, 'col')
- panel_rows: bfloat16 [4, 8, 128, 2048], P('row', 'col')
Inputs may be any that keep to these rules, and one draw needn't show every extreme that they name: `inverse`: zero above the diagonal.
All inputs are finite; a program needn't handle non-finite values.
Results may differ from a plain program's by a relative error of at most 0.0049.
Values may be sent and summed in bfloat16 or wider, within the bound.
A program may use at most 128 MiB of HBM per device.

v0:
```python
import jax
import jax.numpy as jnp
from jax import lax
from jax.sharding import PartitionSpec as P


def gaussian(left_rows, right_rows, inv_scale):
    sq_left = jnp.sum(jnp.square(left_rows.astype(jnp.float32)), axis=-1)
    sq_right = jnp.sum(jnp.square(right_rows.astype(jnp.float32)), axis=-1)
    inner = lax.dot_general(
        left_rows, right_rows, (((1,), (1,)), ((), ())), preferred_element_type=jnp.float32
    )
    return jnp.exp(-inv_scale * (sq_left[:, None] + sq_right[None, :] - 2.0 * inner))


def factor(rows_emb, panel_emb, inverse, inv_scale):
    kernel = gaussian(rows_emb, panel_emb, inv_scale).astype(jnp.bfloat16)
    block_width = inverse.shape[0] // 4
    pieces = []
    for block_at in range(4):
        finish = (block_at + 1) * block_width
        pieces.append(
            lax.dot_general(
                kernel[:, :finish],
                inverse[block_at * block_width : finish, :finish],
                (((1,), (1,)), ((), ())),
                preferred_element_type=jnp.float32,
            )
        )
    return jnp.concatenate(pieces, 1).astype(jnp.bfloat16)


def shards(teacher, panel_ids, rest_ids, inverse):
    n_row = lax.axis_size("row")
    n_col = lax.axis_size("col")
    row_at = lax.axis_index("row")
    col_at = lax.axis_index("col")
    stretch_rows = rest_ids.shape[2]
    inv_scale = 2.0 / teacher.shape[1]
    gathered = lax.all_gather(rest_ids, ("row", "col"), axis=0, tiled=True)
    blocks = gathered.reshape(n_row * n_col, stretch_rows)
    panel = lax.all_gather(panel_ids, "col", axis=0, tiled=True)
    panel_emb = teacher[panel]
    own_ids = lax.dynamic_slice_in_dim(blocks, row_at * n_col + col_at, 1, 0).reshape(stretch_rows)
    col_ids = lax.dynamic_slice_in_dim(
        blocks.reshape(n_row, n_col, stretch_rows), col_at, 1, 1
    ).reshape(-1)
    row_ids = lax.dynamic_slice_in_dim(
        blocks.reshape(n_col, n_row, stretch_rows), row_at, 1, 1
    ).reshape(-1)
    own_factor = factor(teacher[own_ids], panel_emb, inverse, inv_scale)
    col_emb = teacher[col_ids]
    col_factor = lax.all_gather(own_factor, "row", axis=0, tiled=True)
    row_emb = teacher[row_ids]
    kernel = gaussian(row_emb, col_emb, inv_scale)
    row_factor = factor(row_emb, panel_emb, inverse, inv_scale)
    update = lax.dot_general(
        row_factor, col_factor, (((1,), (1,)), ((), ())), preferred_element_type=jnp.float32
    )
    rows_local = jnp.arange(n_col * stretch_rows, dtype=jnp.int32)
    row_index = (
        rows_local // stretch_rows * n_row + row_at
    ) * stretch_rows + rows_local % stretch_rows
    cols_local = jnp.arange(n_row * stretch_rows, dtype=jnp.int32)
    col_index = (
        cols_local // stretch_rows * n_col + col_at
    ) * stretch_rows + cols_local % stretch_rows
    result = kernel - update
    trailing = jnp.where(row_index[:, None] >= col_index[None, :], result, jnp.zeros_like(result))
    return (
        trailing.reshape(n_col, 1, stretch_rows, n_row, 1, stretch_rows),
        own_factor.reshape(1, 1, stretch_rows, own_factor.shape[1]),
    )


def solution(mesh):
    return jax.shard_map(
        shards,
        mesh=mesh,
        in_specs=(P(), P("col"), P("row", "col", None), P()),
        out_specs=(P(None, "row", None, None, "col", None), P("row", "col", None, None)),
        check_vma=False,
    )
```

profile of v0, /device:TPU:0, one launch (start us, length us, event | category | flops | bytes accessed | tf_op | source)
XLA Modules:
  0.0 132.2 jit_solution(9935352924947401463)
XLA Ops:
  7.2 0.0 all-gather.3.cloned.1.call-start
  7.2 43.5 %all_gather.9 = s32[32,1,128]{2,1,0:T(1,128)S(1)} all-gather(s32[1,1,128]{2,1,0:T(1,128)} %param.6), channel_id=1, replica_groups=mesh['row'=4,'col'=8] {'row','col'}, dimensions={0}, use_global_device_ids=true | all-gather | bytes 16896 | tf_op jit(solution)/shard_map/all_gather | solution.py:40
  50.7 5.2 %gather_fusion.3 = bf16[128,256]{1,0:T(8,128)(2,1)S(1)} fusion(bf16[16384,256]{1,0:T(8,128)(2,1)} %param.4, s32[1024]{0:T(1024)S(1)} %pad_clamp_fusion), kind=kCustom, calls=%fused_computation.3 | custom fusion | bytes 131584 | tf_op jit(solution)/shard_map/gather | solution.py:51
  55.9 0.1 multiply_reduce_fusion.3
  56.0 9.0 %all-gather = s32[8,1,256]{2,1,0:T(1,128)S(1)} all-gather(s32[1,1,256]{2,1,0:T(1,128)} %bitcast.42), channel_id=1, replica_groups=mesh['row'=4,'col'=8] {'col'}, dimensions={0}, use_global_device_ids=true | all-gather | bytes 9216 | tf_op jit(solution)/shard_map/all_gather | solution.py:42
  65.0 11.1 %gather_fusion.2 = bf16[2048,256]{1,0:T(8,128)(2,1)S(1)} fusion(bf16[16384,256]{1,0:T(8,128)(2,1)} %param.4, s32[2048]{0:T(1024)S(1)} %fusion.46), kind=kCustom, calls=%fused_computation.2 | custom fusion | bytes 2105344 | tf_op jit(solution)/shard_map/gather | solution.py:43
  76.1 0.3 multiply_reduce_fusion
  76.5 0.5 fusion.13
  77.0 1.3 %convolution_convert_fusion.1 = bf16[128,512]{1,0:T(8,128)(2,1)S(1)} fusion(bf16[2048,2048]{1,0:T(8,128)(2,1)} %param.7, bf16[128,2048]{1,0:T(8,128)(2,1)S(1)} %fusion.13), kind=kOutput, calls=%fused_computation.36 | convolution fusion | flops 67174400 | bytes 786432 | tf_op jit(solution)/shard_map/dot_general | solution.py:23
  78.4 1.7 %convolution_convert_fusion.2 = bf16[128,512]{1,0:T(8,128)(2,1)S(1)} fusion(bf16[2048,2048]{1,0:T(8,128)(2,1)} %param.7, bf16[128,2048]{1,0:T(8,128)(2,1)S(1)} %fusion.13), kind=kOutput, calls=%fused_computation.37 | convolution fusion | flops 134283264 | bytes 1441792 | tf_op jit(solution)/shard_map/dot_general | solution.py:23
  80.1 2.4 %fusion.32 = bf16[128,512]{1,0:T(8,128)(2,1)S(1)} fusion(bf16[128,2048]{1,0:T(8,128)(2,1)S(1)} %fusion.13, bf16[2048,2048]{1,0:T(8,128)(2,1)} %param.7), kind=kOutput, calls=%fused_computation.35 | convolution fusion | flops 268500992 | bytes 2752512 | tf_op jit(solution)/shard_map/dot_general | solution.py:23
  82.5 2.1 %fusion.35 = bf16[128,512]{1,0:T(8,128)(2,1)S(1)} fusion(bf16[2048,2048]{1,0:T(8,128)(2,1)} %param.7, bf16[128,2048]{1,0:T(8,128)(2,1)S(1)} %fusion.13), kind=kOutput, calls=%fused_computation.38 | convolution fusion | flops 201392128 | bytes 2097152 | tf_op jit(solution)/shard_map/dot_general | solution.py:23
  84.6 0.8 pad_maximum_fusion
  85.4 0.0 all-gather.3.cloned.1.call-update
  85.5 7.9 %gather_fusion = bf16[1024,256]{1,0:T(8,128)(2,1)S(1)} fusion(bf16[16384,256]{1,0:T(8,128)(2,1)} %param.4, s32[1024]{0:T(1024)S(1)} %broadcast_clamp_fusion), kind=kCustom, calls=%fused_computation | custom fusion | bytes 1052672 | tf_op jit(solution)/shard_map/gather | solution.py:54
  93.4 6.0 %gather_fusion.1 = bf16[512,256]{1,0:T(8,128)(2,1)S(1)} fusion(bf16[16384,256]{1,0:T(8,128)(2,1)} %param.4, s32[1024]{0:T(1024)S(1)} %pad_clamp_fusion.1), kind=kCustom, calls=%fused_computation.1 | custom fusion | bytes 526336 | tf_op jit(solution)/shard_map/gather | solution.py:52
  99.5 0.1 multiply_reduce_fusion.2
  99.7 0.2 multiply_reduce_fusion.1
  99.9 0.0 slice-start
  99.9 0.8 pad_maximum_fusion.1
  100.7 0.0 slice-start.1
  100.7 2.6 %exponential_convert_fusion = bf16[1024,2048]{1,0:T(8,128)(2,1)S(1)} fusion(bf16[1024,256]{1,0:T(8,128)(2,1)S(1)} %gather_fusion, bf16[2048,256]{1,0:T(8,128)(2,1)S(1)} %gather_fusion.2, f32[2048]{0:T(1024)S(1)} %multiply_reduce_fusion, f32[1024]{0:T(1024)S(1)} %multiply_reduce_fusion.1), kind=kOutput, calls=%fused_computation.4 | convolution fusion | flops 1084227584 | bytes 5779456 | tf_op jit(solution)/shard_map/dot_general | solution.py:10
  103.3 0.0 slice-done
  103.3 0.4 slice-done.1
  103.7 0.7 convolution_convert_fusion
  104.4 1.3 fusion.20
  105.7 2.8 %fusion.23 = bf16[1024,512]{1,0:T(8,128)(2,1)} fusion(bf16[1024,2048]{1,0:T(8,128)(2,1)S(1)} %exponential_convert_fusion, bf16[2048,2048]{1,0:T(8,128)(2,1)S(1)} %bitcast.44), kind=kOutput, calls=%fused_computation.29 | convolution fusion | flops 1611137024 | bytes 5767168 | tf_op jit(solution)/shard_map/dot_general | solution.py:23
  108.5 3.3 %fusion.26 = bf16[1024,512]{1,0:T(8,128)(2,1)} fusion(bf16[1024,2048]{1,0:T(8,128)(2,1)S(1)} %exponential_convert_fusion, bf16[2048,2048]{1,0:T(8,128)(2,1)S(1)} %bitcast.44), kind=kOutput, calls=%fused_computation.31 | convolution fusion | flops 2148007936 | bytes 7340032 | tf_op jit(solution)/shard_map/dot_general | solution.py:23
  111.9 6.3 %all-gather.3.cloned.1.call-done = bf16[512,2048]{1,0:T(8,128)(2,1)} async-done(((bf16[128,2048]{1,0:T(8,128)(2,1)}), bf16[512,2048]{1,0:T(8,128)(2,1)}) %all-gather.3.cloned.1.call-update) | async-done | bytes 2097168 | tf_op jit(solution)/shard_map/all_gather | solution.py:53
  118.2 4.5 %fusion = f32[1024,512]{1,0:T(8,128)S(1)} fusion(bf16[512,2048]{1,0:T(8,128)(2,1)} %all-gather.3.cloned.1.call-done, bf16[1024,512]{1,0:T(8,128)(2,1)} %fusion.26, bf16[1024,512]{1,0:T(8,128)(2,1)} %fusion.23, bf16[1024,512]{1,0:T(8,128)(2,1)S(1)} %fusion.20, bf16[1024,512]{1,0:T(8,128)(2,1)S(1)} %convolution_convert_fusion), kind=kOutput, calls=%fused_computation.5 | convolution fusion | flops 2164260864 | bytes 8388608 | tf_op jit(solution)/shard_map/dot_general | solution.py:57
  122.8 0.8 subtract_select_fusion
  123.6 1.7 %reshape.218 = f32[8,1,128,4,1,128]{5,3,2,0,4,1:T(4,128)} reshape(f32[1024,512]{1,0:T(8,128)S(1)} %subtract_select_fusion) | data formatting | bytes 4194304 | tf_op jit(solution)/shard_map/reshape | solution.py:71
  (10 shorter events, 0.1 us)
Async XLA Ops:
  7.2 111.1 %all-gather.3.cloned.1.call-start = ((), (), s32[]{:S(2)}) async-start(), calls=%async_computation | async-start | bytes 2621440 | tf_op jit(solution)/shard_map/all_gather | solution.py:53
  99.9 3.4 %slice-start = ((s8[8388608]{0:T(1024)(128)(4,1)}), s8[4194304]{0:T(1024)(128)(4,1)S(1)}, s32[]{:S(2)}) async-start(s8[8388608]{0:T(1024)(128)(4,1)} %bitcast.43), calls=%async_computation.1 | async-start | bytes 8388608
  100.7 3.0 %slice-start.1 = ((s8[8388608]{0:T(1024)(128)(4,1)}), s8[4194304]{0:T(1024)(128)(4,1)S(1)}, s32[]{:S(2)}) async-start(s8[8388608]{0:T(1024)(128)(4,1)} %bitcast.43), calls=%async_computation.2 | async-start | bytes 8388608
Sparse Core Ops, SparseCore 0:
  85.6 32.6 all-gather.2
where the time goes:
time: 133 us; the launch traced here: 132 us
  blocking collectives  52.5 us (39%)
  local copies, waits for them, and re-layouts  32.4 us (24%)
  matrix products  24.1 us (18%)
  between operations  14.2 us (11%)
  waiting for transfers between devices  6.36 us (5%)
  other arithmetic  2.57 us (2%)
    all_gather x1, blocking collectives, shards(): gathered = lax.all_gather(rest_ids, ('row', 'col'), axis=0, tiled=True)  43.5 us
    dot_general x8, matrix products, factor(): lax.dot_general(kernel[:, :finish], inverse[block_at * block_width:finish...  15.7 us
    gather x1, local copies, waits for them, and re-layouts, shards(): panel_emb = teacher[panel]  11.1 us
    all_gather x1, blocking collectives, shards(): panel = lax.all_gather(panel_ids, 'col', axis=0, tiled=True)  8.99 us
    gather x1, local copies, waits for them, and re-layouts, shards(): row_emb = teacher[row_ids]  7.92 us
    all_gather x1, waiting for transfers between devices, shards(): col_factor = lax.all_gather(own_factor, 'row', axis=0, tiled=True)  6.34 us
    gather x1, local copies, waits for them, and re-layouts, shards(): col_emb = teacher[col_ids]  6.02 us
    gather x1, local copies, waits for them, and re-layouts, shards(): own_factor = factor(teacher[own_ids], panel_emb, inverse, inv_scale)  5.22 us
  transfers between devices with their start and end apart: 1, of which 1 were waited for; matrix products, arithmetic and copies ran while one was open for 20% of the time, Pallas kernels for 0%

commit v1 on v0

--- a/solution.py
+++ b/solution.py
@@ -39,7 +39,22 @@
     inv_scale = 2.0 / teacher.shape[1]
     gathered = lax.all_gather(rest_ids, ("row", "col"), axis=0, tiled=True)
     blocks = gathered.reshape(n_row * n_col, stretch_rows)
-    panel = lax.all_gather(panel_ids, "col", axis=0, tiled=True)
+    full_n = lax.axis_size("col")
+    made = []
+    for k in range(full_n):
+        made.append((k, (k + 1) % full_n))
+    trail = []
+    for k in range(full_n):
+        trail.append((k, (k - 1) % full_n))
+    new, f_next = ([panel_ids], [panel_ids])
+    for _ in range(full_n // 2):
+        outcome_arr = lax.ppermute(new[-1], "col", made)
+        new.append(outcome_arr)
+    for _ in range((full_n - 1) // 2):
+        res = lax.ppermute(f_next[-1], "col", trail)
+        f_next.append(res)
+    work_now = jnp.concatenate([*new[::-1], *f_next[1:]], axis=0)
+    panel = jnp.roll(work_now, (lax.axis_index("col") - full_n // 2) * panel_ids.shape[0], axis=0)
     panel_emb = teacher[panel]
     own_ids = lax.dynamic_slice_in_dim(blocks, row_at * n_col + col_at, 1, 0).reshape(stretch_rows)
     col_ids = lax.dynamic_slice_in_dim(

time: 133 us -> 150 us (1.13)
  waiting for transfers between devices: 6.36 us -> 22.8 us
  starting transfers between devices: 0.04 us -> 12.2 us
  blocking collectives: 52.5 us -> 40.6 us
    ppermute x0 -> x7, starting transfers between devices: none -> 12.2 us  [the longest x3 11.3 us: shards(): res = lax.ppermute(f_next[-1], 'col', trail)]
    all_gather x1, waiting for transfers between devices: 6.34 us -> 16 us  [shards(): col_factor = lax.all_gather(own_factor, 'row', axis=0, tiled=True)]
    all_gather x1 -> x0, blocking collectives: 8.99 us -> none  [shards(): panel = lax.all_gather(panel_ids, 'col', axis=0, tiled=True)]
    ppermute x0 -> x7, waiting for transfers between devices: none -> 6.75 us  [the longest x4 5.54 us: shards(): outcome_arr = lax.ppermute(new[-1], 'col', made)]
    all_gather x1, blocking collectives: 43.5 us -> 40.6 us  [shards(): gathered = lax.all_gather(rest_ids, ('row', 'col'), axis=0, tiled=True)]
  transfers between devices with their start and end apart: 1 -> 8, of which waited for: 1 -> 4; matrix products, arithmetic and copies ran while one was open for 20% -> 21% of each run, Pallas kernels for 0% -> 0%
where the time goes in v1:
time: 150 us
  blocking collectives  40.6 us (27%)
  local copies, waits for them, and re-layouts  33 us (22%)
  matrix products  24 us (16%)
  waiting for transfers between devices  22.8 us (15%)
  between operations  14.4 us (10%)
  starting transfers between devices  12.2 us (8%)
  other arithmetic  2.64 us (2%)
    all_gather x1, blocking collectives, shards(): gathered = lax.all_gather(rest_ids, ('row', 'col'), axis=0, tiled=True)  40.6 us
    all_gather x1, waiting for transfers between devices, shards(): col_factor = lax.all_gather(own_factor, 'row', axis=0, tiled=True)  16 us
    dot_general x8, matrix products, factor(): lax.dot_general(kernel[:, :finish], inverse[block_at * block_width:finish...  15.7 us
    gather x1, local copies, waits for them, and re-layouts, shards(): panel_emb = teacher[panel]  11.3 us
    ppermute x3, starting transfers between devices, shards(): res = lax.ppermute(f_next[-1], 'col', trail)  11.3 us
    gather x1, local copies, waits for them, and re-layouts, shards(): row_emb = teacher[row_ids]  7.92 us
    gather x1, local copies, waits for them, and re-layouts, shards(): col_emb = teacher[col_ids]  6.02 us
    ppermute x4, waiting for transfers between devices, shards(): outcome_arr = lax.ppermute(new[-1], 'col', made)  5.54 us
  transfers between devices with their start and end apart: 8, of which 4 were waited for; matrix products, arithmetic and copies ran while one was open for 21% of the time, Pallas kernels for 0%

profile of v1, /device:TPU:0, one launch (start us, length us, event | category | flops | bytes accessed | tf_op | source)
XLA Modules:
  0.0 149.6 jit_solution(6067839753580586553)
XLA Ops:
  7.2 0.5 collective-permute-start
  7.8 4.1 %collective-permute-start.4 = (s32[256]{0:T(256)}, s32[256]{0:T(256)S(1)}, u32[]{:S(2)}, u32[]{:S(2)}) collective-permute-start(s32[256]{0:T(256)} %param.5), channel_id=1, source_target_pairs={{0,7},{1,0},{2,1},{3,2},{4,3},{5,4},{6,5},{7,6},{8,15},{9,8},{10,9... | collective-permute-start | bytes 3080 | tf_op jit(solution)/shard_map/ppermute | solution.py:54
  11.9 40.6 %all_gather.6 = s32[32,1,128]{2,1,0:T(1,128)S(1)} all-gather(s32[1,1,128]{2,1,0:T(1,128)} %param.6), channel_id=1, replica_groups=mesh['row'=4,'col'=8] {'row','col'}, dimensions={0}, use_global_device_ids=true | all-gather | bytes 16896 | tf_op jit(solution)/shard_map/all_gather | solution.py:40
  52.5 5.2 %gather_fusion.3 = bf16[128,256]{1,0:T(8,128)(2,1)S(1)} fusion(bf16[16384,256]{1,0:T(8,128)(2,1)} %param.4, s32[1024]{0:T(1024)S(1)} %pad_clamp_fusion), kind=kCustom, calls=%fused_computation.3 | custom fusion | bytes 131584 | tf_op jit(solution)/shard_map/gather | solution.py:66
  57.8 0.4 collective-permute-start.1
  58.3 4.3 %collective-permute-done.1 = s32[256]{0:T(256)S(1)} collective-permute-done((s32[256]{0:T(256)S(1)}, s32[256]{0:T(256)S(1)}, u32[]{:S(2)}, u32[]{:S(2)}) %collective-permute-start.1) | collective-permute-done | bytes 1056 | tf_op jit(solution)/shard_map/ppermute | solution.py:51
  62.6 3.6 %collective-permute-start.5 = (s32[256]{0:T(256)S(1)}, s32[256]{0:T(256)S(1)}, u32[]{:S(2)}, u32[]{:S(2)}) collective-permute-start(s32[256]{0:T(256)S(1)} %collective-permute-done.4), channel_id=1, source_target_pairs={{0,7},{1,0},{2,1},{3,2},{4,3},{5,4},{6,5},{7,6},{8,15},{9,8},{10,9... | collective-permute-start | bytes 3080 | tf_op jit(solution)/shard_map/ppermute | solution.py:54
  66.2 1.2 collective-permute-done.2
  67.4 7.9 %gather_fusion = bf16[1024,256]{1,0:T(8,128)(2,1)S(1)} fusion(bf16[16384,256]{1,0:T(8,128)(2,1)} %param.4, s32[1024]{0:T(1024)S(1)} %broadcast_clamp_fusion), kind=kCustom, calls=%fused_computation | custom fusion | bytes 1052672 | tf_op jit(solution)/shard_map/gather | solution.py:69
  75.4 3.6 %collective-permute-start.6 = (s32[256]{0:T(256)S(1)}, s32[256]{0:T(256)S(1)}, u32[]{:S(2)}, u32[]{:S(2)}) collective-permute-start(s32[256]{0:T(256)S(1)} %collective-permute-done.5), channel_id=1, source_target_pairs={{0,7},{1,0},{2,1},{3,2},{4,3},{5,4},{6,5},{7,6},{8,15},{9,8},{10,9... | collective-permute-start | bytes 3080 | tf_op jit(solution)/shard_map/ppermute | solution.py:54
  79.1 1.2 collective-permute-done.6
  80.4 11.3 %gather_fusion.2 = bf16[2048,256]{1,0:T(8,128)(2,1)S(1)} fusion(bf16[16384,256]{1,0:T(8,128)(2,1)} %param.4, s32[2048]{0:T(1024)S(1)} %fusion.46), kind=kCustom, calls=%fused_computation.2 | custom fusion | bytes 2105344 | tf_op jit(solution)/shard_map/gather | solution.py:58
  91.7 0.3 multiply_reduce_fusion
  92.1 0.5 fusion.13
  92.6 1.3 convolution_convert_fusion.1
  94.0 1.7 %convolution_convert_fusion.2 = bf16[128,512]{1,0:T(8,128)(2,1)S(1)} fusion(bf16[2048,2048]{1,0:T(8,128)(2,1)} %param.7, bf16[128,2048]{1,0:T(8,128)(2,1)S(1)} %fusion.13), kind=kOutput, calls=%fused_computation.37 | convolution fusion | flops 134283264 | bytes 1441792 | tf_op jit(solution)/shard_map/dot_general | solution.py:23
  95.7 2.4 %fusion.32 = bf16[128,512]{1,0:T(8,128)(2,1)S(1)} fusion(bf16[128,2048]{1,0:T(8,128)(2,1)S(1)} %fusion.13, bf16[2048,2048]{1,0:T(8,128)(2,1)} %param.7), kind=kOutput, calls=%fused_computation.35 | convolution fusion | flops 268500992 | bytes 2752512 | tf_op jit(solution)/shard_map/dot_general | solution.py:23
  98.1 2.1 %fusion.35 = bf16[128,512]{1,0:T(8,128)(2,1)S(1)} fusion(bf16[2048,2048]{1,0:T(8,128)(2,1)} %param.7, bf16[128,2048]{1,0:T(8,128)(2,1)S(1)} %fusion.13), kind=kOutput, calls=%fused_computation.38 | convolution fusion | flops 201392128 | bytes 2097152 | tf_op jit(solution)/shard_map/dot_general | solution.py:23
  100.2 0.8 pad_maximum_fusion
  101.0 6.0 %gather_fusion.1 = bf16[512,256]{1,0:T(8,128)(2,1)S(1)} fusion(bf16[16384,256]{1,0:T(8,128)(2,1)} %param.4, s32[1024]{0:T(1024)S(1)} %pad_clamp_fusion.1), kind=kCustom, calls=%fused_computation.1 | custom fusion | bytes 526336 | tf_op jit(solution)/shard_map/gather | solution.py:67
  107.3 0.2 multiply_reduce_fusion.1
  107.5 0.8 pad_maximum_fusion.1
  108.3 2.4 %exponential_convert_fusion = bf16[1024,2048]{1,0:T(8,128)(2,1)S(1)} fusion(bf16[1024,256]{1,0:T(8,128)(2,1)S(1)} %gather_fusion, bf16[2048,256]{1,0:T(8,128)(2,1)S(1)} %gather_fusion.2, f32[2048]{0:T(1024)S(1)} %multiply_reduce_fusion, f32[1024]{0:T(1024)S(1)} %multiply_reduce_fusion.1), kind=kOutput, calls=%fused_computation.4 | convolution fusion | flops 1084227584 | bytes 5779456 | tf_op jit(solution)/shard_map/dot_general | solution.py:10
  110.7 0.7 slice-done.1
  111.5 0.7 convolution_convert_fusion
  112.2 1.3 fusion.20
  113.5 2.8 %fusion.23 = bf16[1024,512]{1,0:T(8,128)(2,1)} fusion(bf16[1024,2048]{1,0:T(8,128)(2,1)S(1)} %exponential_convert_fusion, bf16[2048,2048]{1,0:T(8,128)(2,1)S(1)} %bitcast.40), kind=kOutput, calls=%fused_computation.29 | convolution fusion | flops 1611137024 | bytes 5767168 | tf_op jit(solution)/shard_map/dot_general | solution.py:23
  116.3 3.3 %fusion.26 = bf16[1024,512]{1,0:T(8,128)(2,1)} fusion(bf16[1024,2048]{1,0:T(8,128)(2,1)S(1)} %exponential_convert_fusion, bf16[2048,2048]{1,0:T(8,128)(2,1)S(1)} %bitcast.40), kind=kOutput, calls=%fused_computation.31 | convolution fusion | flops 2148007936 | bytes 7340032 | tf_op jit(solution)/shard_map/dot_general | solution.py:23
  119.6 16.0 %all-gather.2.cloned.1.call-done = bf16[512,2048]{1,0:T(8,128)(2,1)} async-done(((bf16[128,2048]{1,0:T(8,128)(2,1)}), bf16[512,2048]{1,0:T(8,128)(2,1)}) %all-gather.2.cloned.1.call-update) | async-done | bytes 2097168 | tf_op jit(solution)/shard_map/all_gather | solution.py:68
  135.7 4.5 %fusion = f32[1024,512]{1,0:T(8,128)S(1)} fusion(bf16[512,2048]{1,0:T(8,128)(2,1)} %all-gather.2.cloned.1.call-done, bf16[1024,512]{1,0:T(8,128)(2,1)} %fusion.26, bf16[1024,512]{1,0:T(8,128)(2,1)} %fusion.23, bf16[1024,512]{1,0:T(8,128)(2,1)S(1)} %fusion.20, bf16[1024,512]{1,0:T(8,128)(2,1)S(1)} %convolution_convert_fusion), kind=kOutput, calls=%fused_computation.5 | convolution fusion | flops 2164260864 | bytes 8388608 | tf_op jit(solution)/shard_map/dot_general | solution.py:72
  140.2 0.8 subtract_select_fusion
  141.0 1.7 %reshape.218 = f32[8,1,128,4,1,128]{5,3,2,0,4,1:T(4,128)} reshape(f32[1024,512]{1,0:T(8,128)S(1)} %subtract_select_fusion) | data formatting | bytes 4194304 | tf_op jit(solution)/shard_map/reshape | solution.py:86
  (42 shorter events, 0.6 us)
Async XLA Ops:
  7.2 71.8 %copy-start = (s32[256]{0:T(256)S(1)}, s32[256]{0:T(256)}, u32[]{:S(2)}) copy-start(s32[256]{0:T(256)} %param.5) | copy-start | bytes 3076
  7.2 128.5 %all-gather.2.cloned.1.call-start = ((), (), s32[]{:S(2)}) async-start(), calls=%async_computation | async-start | bytes 2621440 | tf_op jit(solution)/shard_map/all_gather | solution.py:68
  7.2 50.5 %collective-permute-start = (s32[256]{0:T(256)}, s32[256]{0:T(256)S(1)}, u32[]{:S(2)}, u32[]{:S(2)}) collective-permute-start(s32[256]{0:T(256)} %param.5), channel_id=1, source_target_pairs={{0,1},{1,2},{2,3},{3,4},{4,5},{5,6},{6,7},{7,0},{8,9},{9,10},{10,1... | collective-permute-start | bytes 3080 | tf_op jit(solution)/shard_map/ppermute | solution.py:51
  7.8 54.9 %collective-permute-start.4 = (s32[256]{0:T(256)}, s32[256]{0:T(256)S(1)}, u32[]{:S(2)}, u32[]{:S(2)}) collective-permute-start(s32[256]{0:T(256)} %param.5), channel_id=1, source_target_pairs={{0,7},{1,0},{2,1},{3,2},{4,3},{5,4},{6,5},{7,6},{8,15},{9,8},{10,9... | collective-permute-start | bytes 3080 | tf_op jit(solution)/shard_map/ppermute | solution.py:54
  57.8 4.8 %collective-permute-start.1 = (s32[256]{0:T(256)S(1)}, s32[256]{0:T(256)S(1)}, u32[]{:S(2)}, u32[]{:S(2)}) collective-permute-start(s32[256]{0:T(256)S(1)} %collective-permute-done), channel_id=1, source_target_pairs={{0,1},{1,2},{2,3},{3,4},{4,5},{5,6},{6,7},{7,0},{8,9},{9,10},{10,1... | collective-permute-start | bytes 3080 | tf_op jit(solution)/shard_map/ppermute | solution.py:51
  62.6 4.8 %collective-permute-start.2 = (s32[256]{0:T(256)S(1)}, s32[256]{0:T(256)S(1)}, u32[]{:S(2)}, u32[]{:S(2)}) collective-permute-start(s32[256]{0:T(256)S(1)} %collective-permute-done.1), channel_id=1, source_target_pairs={{0,1},{1,2},{2,3},{3,4},{4,5},{5,6},{6,7},{7,0},{8,9},{9,10},{10,1... | collective-permute-start | bytes 3080 | tf_op jit(solution)/shard_map/ppermute | solution.py:51
  62.6 12.7 %collective-permute-start.5 = (s32[256]{0:T(256)S(1)}, s32[256]{0:T(256)S(1)}, u32[]{:S(2)}, u32[]{:S(2)}) collective-permute-start(s32[256]{0:T(256)S(1)} %collective-permute-done.4), channel_id=1, source_target_pairs={{0,7},{1,0},{2,1},{3,2},{4,3},{5,4},{6,5},{7,6},{8,15},{9,8},{10,9... | collective-permute-start | bytes 3080 | tf_op jit(solution)/shard_map/ppermute | solution.py:54
  67.4 11.5 %collective-permute-start.3 = (s32[256]{0:T(256)S(1)}, s32[256]{0:T(256)S(1)}, u32[]{:S(2)}, u32[]{:S(2)}) collective-permute-start(s32[256]{0:T(256)S(1)} %collective-permute-done.2), channel_id=1, source_target_pairs={{0,1},{1,2},{2,3},{3,4},{4,5},{5,6},{6,7},{7,0},{8,9},{9,10},{10,1... | collective-permute-start | bytes 3080 | tf_op jit(solution)/shard_map/ppermute | solution.py:51
  75.4 4.9 %collective-permute-start.6 = (s32[256]{0:T(256)S(1)}, s32[256]{0:T(256)S(1)}, u32[]{:S(2)}, u32[]{:S(2)}) collective-permute-start(s32[256]{0:T(256)S(1)} %collective-permute-done.5), channel_id=1, source_target_pairs={{0,7},{1,0},{2,1},{3,2},{4,3},{5,4},{6,5},{7,6},{8,15},{9,8},{10,9... | collective-permute-start | bytes 3080 | tf_op jit(solution)/shard_map/ppermute | solution.py:54
  107.5 3.2 %slice-start = ((s8[8388608]{0:T(1024)(128)(4,1)}), s8[4194304]{0:T(1024)(128)(4,1)S(1)}, s32[]{:S(2)}) async-start(s8[8388608]{0:T(1024)(128)(4,1)} %bitcast.39), calls=%async_computation.1 | async-start | bytes 8388608
  108.3 3.1 %slice-start.1 = ((s8[8388608]{0:T(1024)(128)(4,1)}), s8[4194304]{0:T(1024)(128)(4,1)S(1)}, s32[]{:S(2)}) async-start(s8[8388608]{0:T(1024)(128)(4,1)} %bitcast.39), calls=%async_computation.2 | async-start | bytes 8388608
Sparse Core Ops, SparseCore 0:
  101.2 34.4 all-gather.1
